TPU v7x, 512 devices: a whole 4x4x16 slice. The times are simulated.
512 devices in a mesh: dp: 128 (over x_hi, y, z), fsdp: 4 (over x_lo, core).
Axes of the slice: x: 4 (x_hi: 2, x_lo: 2; x = x_hi * 2 + x_lo), y: 4, z: 16, core: 2. Of those that a mesh axis runs over, the one named last changes fastest.
Arguments:
- tokens: bfloat16 [65536, 1280], P(('dp', 'fsdp')), may hold values from -3 to 3
- qkv_weight: bfloat16 [3, 1280, 1280], P(None, 'dp', 'fsdp'), may hold values from -1 to 1
- out_weight: bfloat16 [1280, 1280], P('fsdp', 'dp'), may hold values from -0.15625 to 0.15625
- merge_weight: bfloat16 [5120, 1280], P(('dp', 'fsdp')), may hold values from -0.078125 to 0.078125
- ln_gains: float32 [2, 1280], replicated, may hold values from 0.25 to 1.75
- segments: int32 [128, 512], P('dp', 'fsdp'), may hold values from 0 to 2, never falling along the last dimension, each value on 1 to 256 neighbouring positions
- merge_rows: int32 [512, 128], P(('dp', 'fsdp')), may hold values from 0 to 127, each once within a row
- owners: int32 [16384, 1], P(('dp', 'fsdp')), may hold values from 0 to 127; in each aligned block of 32 rows (0 to 31, 32 to 63, ...) at most 2 rows name the same one
Outputs:
- owned: bfloat16 [131072, 1280], P(('dp', 'fsdp'))
Inputs may be any that keep to these rules, and one draw needn't show every extreme that they name: `segments`: within each row segment numbers never fall, every number appears, each request has 1 to 256 tokens and one has exactly 256. `merge_rows`: each row is a permutation of the device's local rows. `owners`: among the 32 merged tokens of one device no owner appears more than 2 times, and in some devices one appears exactly 2 times.
All inputs are finite; a program needn't handle non-finite values.
Results may differ from a plain program's by a relative error of at most 0.02.
Values may be sent and summed in bfloat16 or wider, within the bound.
A program may use at most 64 MiB of HBM per device.

v0:
```python
import math
import jax
import jax.numpy as jnp
from jax import lax
from jax.sharding import PartitionSpec as P

HD = 80
epsilon = 1e-06


def normalize(values_in, gain_row):
    widened = values_in.astype(jnp.float32)
    centered = widened - jnp.mean(widened, axis=1, keepdims=True)
    variance = jnp.mean(centered * centered, axis=1, keepdims=True)
    return (centered * lax.rsqrt(variance + epsilon) * gain_row).astype(jnp.bfloat16)


def attend(queries, keys_all, values_all, seg_rows, seg_cols):
    factor = 1.0 / math.sqrt(HD)
    allowed = seg_rows[:, None] == seg_cols[None, :]
    pieces = []
    for head_index in range(queries.shape[1] // HD):
        first_col = head_index * HD
        last_col = first_col + HD
        scores = (
            lax.dot_general(
                queries[:, first_col:last_col],
                keys_all[:, first_col:last_col],
                (((1,), (1,)), ((), ())),
                preferred_element_type=jnp.float32,
            )
            * factor
        )
        masked = jnp.where(allowed, scores, -jnp.inf)
        highest = jnp.max(masked, axis=1, keepdims=True)
        weights = jnp.exp(masked - highest)
        totals = jnp.sum(weights, axis=1, keepdims=True)
        head_out = jnp.dot(
            weights.astype(jnp.bfloat16),
            values_all[:, first_col:last_col],
            preferred_element_type=jnp.float32,
        )
        pieces.append(head_out / totals)
    return jnp.concatenate(pieces, axis=1).astype(jnp.bfloat16)


def per_device(
    tokens, qkv_weight, out_weight, merge_weight, ln_gains, segments, merge_rows, owners
):
    n_dp = lax.axis_size("dp")
    n_fsdp = lax.axis_size("fsdp")
    qkv_mine = lax.all_gather(qkv_weight, "dp", axis=1, tiled=True)
    out_mine = lax.all_gather(out_weight, "dp", axis=1, tiled=True)
    normed = normalize(tokens, ln_gains[0])
    group_normed, group_segs = (
        lax.all_gather(normed, "fsdp", axis=0, tiled=True),
        lax.all_gather(segments, "fsdp", axis=1, tiled=True),
    )
    queries = jnp.dot(group_normed, qkv_mine[0], preferred_element_type=jnp.float32).astype(
        jnp.bfloat16
    )
    keys_all = jnp.dot(group_normed, qkv_mine[1], preferred_element_type=jnp.float32).astype(
        jnp.bfloat16
    )
    values_all = jnp.dot(group_normed, qkv_mine[2], preferred_element_type=jnp.float32).astype(
        jnp.bfloat16
    )
    attended_mine = attend(queries, keys_all, values_all, group_segs[0], group_segs[0])
    attended_local = lax.all_to_all(attended_mine, "fsdp", split_axis=0, concat_axis=1, tiled=True)
    out_full = lax.all_gather(out_mine, "fsdp", axis=0, tiled=True)
    update = jnp.dot(attended_local, out_full, preferred_element_type=jnp.float32)
    layer_out = (tokens.astype(jnp.float32) + update).astype(jnp.bfloat16)
    merge_in = normalize(layer_out, ln_gains[1])
    merge_count = tokens.shape[0] // 4
    stacked = jnp.take(merge_in, merge_rows[0], axis=0).reshape(merge_count, 4 * merge_in.shape[1])
    slice_rows = merge_weight.shape[0]
    part_rows = lax.all_gather(merge_weight, "dp", axis=0, tiled=True)
    blocks = stacked.reshape(merge_count, n_dp, n_fsdp * slice_rows)
    received = lax.all_to_all(blocks, "fsdp", split_axis=2, concat_axis=0, tiled=True)
    gathered_inputs = received.reshape(n_fsdp * merge_count, n_dp * slice_rows)
    merged = lax.psum_scatter(
        jnp.dot(gathered_inputs, part_rows, preferred_element_type=jnp.float32).astype(
            jnp.bfloat16
        ),
        "fsdp",
        scatter_dimension=0,
        tiled=True,
    )
    capacity = max(2, (2 * merge_count + n_dp - 1) // n_dp)
    targets = owners[:, 0]
    onehot = (targets[:, None] == jnp.arange(n_dp, dtype=jnp.int32)[None, :]).astype(jnp.int32)
    earlier = jnp.cumsum(onehot, axis=0) - onehot
    position = jnp.sum(earlier * onehot, axis=1)
    slot_index = targets * capacity + position
    placing = (jnp.arange(n_dp * capacity, dtype=jnp.int32)[:, None] == slot_index[None, :]).astype(
        jnp.bfloat16
    )
    packed = jnp.dot(placing, merged, preferred_element_type=jnp.float32).astype(jnp.bfloat16)
    packed = packed.reshape(n_dp, capacity, merged.shape[1])
    arrived = lax.all_to_all(packed, "dp", split_axis=0, concat_axis=0, tiled=True)
    return arrived.reshape(n_dp * capacity, merged.shape[1])


def solution(mesh):
    return jax.shard_map(
        per_device,
        mesh=mesh,
        in_specs=(
            P(("dp", "fsdp"), None),
            P(None, "dp", "fsdp"),
            P("fsdp", "dp"),
            P(("dp", "fsdp"), None),
            P(),
            P("dp", "fsdp"),
            P(("dp", "fsdp"), None),
            P(("dp", "fsdp"), None),
        ),
        out_specs=P(("dp", "fsdp"), None),
        check_vma=False,
    )
```

profile of v0, /device:TPU:32, one launch (start us, length us, event | category | flops | bytes accessed | tf_op | source)
XLA Modules:
  0.0 750.7 jit_solution(5897725297791308447)
XLA Ops:
  6.5 0.7 all-gather.9.cloned.1.call-update
  7.3 0.8 slice_reduce_fusion
  8.1 1.1 convert_reduce_fusion
  9.2 1.2 fusion.23
  10.4 1.9 fusion.25
  12.4 364.9 %all-gather = bf16[128,10,320]{2,1,0:T(8,128)(2,1)S(1)} all-gather(bf16[1,10,320]{2,1,0:T(8,128)(2,1)} %bitcast.57), channel_id=1, replica_groups=mesh['dp'=128,'fsdp'=4] {'dp'}, dimensions={0}, use_global_device_ids=true | all-gather | bytes 825600 | tf_op jit(solution)/shard_map/all_gather | solution.py:53
  377.3 0.6 reshape.112
  378.0 1.3 copy.23
  379.4 0.5 all-gather.13.cloned.1.call-update
  379.9 5.0 all_gather.18
  384.9 0.5 broadcast.113
  385.5 0.6 reduce.7
  386.5 10.5 %fusion.49 = (bf16[1,1280,320]{2,0,1:T(2,128)(2,1)S(1)}, bf16[1,1280,320]{2,0,1:T(2,128)(2,1)}, bf16[1,1280,320]{2,0,1:T(2,128)(2,1)}) fusion(bf16[3,1280,320]{2,0,1:T(4,128)(2,1)} %all-gather.9.cloned.1.call-done), kind=kLoop, calls=%fused_computation.92 | loop fusion | bytes 4915200 | tf_op jit(solution)/shard_map/slice | solution.py:65
  396.9 4.9 copy.28
  401.8 4.9 copy.27
  406.7 2.8 copy.26
  409.5 2.3 convolution_convert_fusion.3
  411.9 0.6 convolution_convert_fusion.4
  412.5 0.4 fusion.53
  413.1 0.4 fusion.52
  413.6 0.4 fusion.51
  414.2 0.4 fusion.50
  414.8 0.6 convolution_convert_fusion.2
  415.4 0.3 fusion.9
  415.7 0.3 fusion.8
  416.0 0.3 fusion.7
  416.3 0.3 fusion.6
  416.7 0.7 pad_maximum_fusion
  417.5 3.5 all-to-all-start
  420.9 0.2 reduce-scatter.2.cloned.1.call-start
  421.2 6.4 all-to-all-done
  427.6 2.6 fusion.54
  430.3 0.2 multiply_reduce_fusion
  430.7 0.9 gather_fusion
  431.6 1.9 gather.7
  433.5 0.7 broadcast_select_fusion
  434.2 0.6 copy.24
  434.8 9.1 %all_to_all.36 = bf16[32,128,40]{1,0,2:T(8,128)(2,1)S(1)} all-to-all(bf16[32,128,40]{1,0,2:T(8,128)(2,1)S(1)} %copy.24), channel_id=1, replica_groups=mesh['dp'=128,'fsdp'=4] {'fsdp'}, dimensions={2} | all-to-all | bytes 655360 | tf_op jit(solution)/shard_map/all_to_all | solution.py:79
  443.9 0.8 copy.25
  444.7 1.4 reshape.100
  446.1 210.0 %all-gather.13.cloned.1.call-done = bf16[128,10,1280]{2,1,0:T(8,128)(2,1)} async-done(((bf16[1,10,1280]{2,1,0:T(8,128)(2,1)}), bf16[128,10,1280]{2,1,0:T(8,128)(2,1)}) %all-gather.13.cloned.1.call-update) | async-done | bytes 3276816 | tf_op jit(solution)/shard_map/all_gather | solution.py:77
  656.1 5.3 reshape.114
  661.4 2.3 convolution_convert_fusion.1
  664.1 19.2 %reduce-scatter.2.cloned.1.call-done = bf16[32,1280]{1,0:T(8,128)(2,1)} async-done(((bf16[128,1280]{1,0:T(8,128)(2,1)}), bf16[32,1280]{1,0:T(8,128)(2,1)}) %reduce-scatter.2.cloned.1.call-update) | async-done | bytes 81936 | tf_op jit(solution)/shard_map/reduce_scatter | solution.py:81
  683.3 1.2 convolution_convert_fusion
  684.5 0.2 reshape.101
  684.7 58.4 %all_to_all.37 = bf16[128,2,1280]{2,1,0:T(2,128)(2,1)S(1)} all-to-all(bf16[128,2,1280]{2,1,0:T(2,128)(2,1)S(1)} %reshape.101), channel_id=1, replica_groups=mesh['dp'=128,'fsdp'=4] {'dp'}, dimensions={0} | all-to-all | bytes 1310720 | tf_op jit(solution)/shard_map/all_to_all | solution.py:100
  743.1 1.1 reshape.102
  (43 shorter events, 1.9 us)
Async XLA Ops:
  6.5 379.9 %all-gather.9.cloned.1.call-start = ((), (), s32[]{:S(2)}) async-start(), calls=%async_computation.5 | async-start | bytes 3962880 | tf_op jit(solution)/shard_map/all_gather | solution.py:52
  7.3 402.2 %all-gather.7.cloned.1.call-start = ((), (), s32[]{:S(2)}) async-start(), calls=%async_computation.4 | async-start | bytes 1638400 | tf_op jit(solution)/shard_map/all_gather | solution.py:56
  12.4 408.8 %all-gather.11.cloned.1.call-start = ((), (), s32[]{:S(2)}) async-start(), calls=%async_computation.6 | async-start | bytes 4096000 | tf_op jit(solution)/shard_map/all_gather | solution.py:70
  378.0 1.9 copy-start.3
  378.0 7.5 copy-start.5
  379.3 276.8 %all-gather.13.cloned.1.call-start = ((), (), s32[]{:S(2)}) async-start(), calls=%async_computation.8 | async-start | bytes 5283840 | tf_op jit(solution)/shard_map/all_gather | solution.py:77
  409.4 2.4 copy-start.1
  409.5 2.4 copy-start.4
  416.0 11.6 %copy-start = (bf16[128,1280]{1,0:T(8,128)(2,1)S(1)}, bf16[128,1280]{1,0:T(8,128)(2,1)}, u32[]{:S(2)}) copy-start(bf16[128,1280]{1,0:T(8,128)(2,1)} %param.8) | copy-start | bytes 983044
  417.5 10.2 %all-to-all-start = ((bf16[4,128,320]{1,2,0:T(8,128)(2,1)}), bf16[4,128,320]{1,2,0:T(8,128)(2,1)S(1)}, u32[]{:S(2)}, u32[]{:S(2)}) async-start(bf16[4,128,320]{1,2,0:T(8,128)(2,1)} %pad_maximum_fusion), calls=%async_computation | async-start | bytes 655360 | tf_op jit(solution)/shard_map/all_to_all | solution.py:69
  420.9 262.3 %reduce-scatter.2.cloned.1.call-start = ((), (), s32[]{:S(2)}) async-start(), calls=%async_computation.7 | async-start | bytes 409600 | tf_op jit(solution)/shard_map/reduce_scatter | solution.py:81
  661.4 2.4 copy-start.2
Sparse Core Ops, SparseCore 0:
  11.8 226.8 all-gather.8
  240.8 25.3 all-gather.6
  379.4 39.2 all-gather.10
  422.9 233.0 all-gather.12
  663.8 19.3 reduce-scatter.1
where the time goes:
time: 752 us; the launch traced here: 751 us
  blocking collectives  437 us (58%)
  waiting for transfers between devices  237 us (32%)
  local copies, waits for them, and re-layouts  38.7 us (5%)
  between operations  13.5 us (2%)
  matrix products  12.4 us (2%)
  other arithmetic  7.87 us (1%)
    all_gather x1, blocking collectives, per_device(): out_mine = lax.all_gather(out_weight, 'dp', axis=1, tiled=True)  365 us
    all_gather x1, waiting for transfers between devices, per_device(): part_rows = lax.all_gather(merge_weight, 'dp', axis=0, tiled=True)  210 us
    all_to_all x1, blocking collectives, per_device(): lax.all_to_all(packed, 'dp', split_axis=0, concat_axis=0, tiled=True)  58.4 us
    unnamed x19, local copies, waits for them, and re-layouts  20.2 us
    reduce_scatter x1, waiting for transfers between devices, per_device(): lax.psum_scatter(jnp.dot(gathered_inputs, part_rows, preferred_element_ty...  19.2 us
  transfers between devices with their start and end apart: 6, of which 3 were waited for; matrix products, arithmetic and copies ran while one was open for 7% of the time, Pallas kernels for 0%

commit v1 on v0

--- a/solution.py
+++ b/solution.py
@@ -50,7 +50,9 @@
     n_dp = lax.axis_size("dp")
     n_fsdp = lax.axis_size("fsdp")
     qkv_mine = lax.all_gather(qkv_weight, "dp", axis=1, tiled=True)
-    out_mine = lax.all_gather(out_weight, "dp", axis=1, tiled=True)
+    out_mine = jnp.concatenate(
+        lax.all_to_all(jnp.stack([out_weight] * lax.axis_size("dp")), "dp", 0, 0), axis=1
+    )
     normed = normalize(tokens, ln_gains[0])
     group_normed, group_segs = (
         lax.all_gather(normed, "fsdp", axis=0, tiled=True),

time: 752 us -> 659 us (0.88)
  blocking collectives: 437 us -> 63.4 us
  waiting for transfers between devices: 237 us -> 491 us
  starting transfers between devices: 3.8 us -> 29.7 us
    all_gather x1 -> x0, blocking collectives: 365 us -> none  [per_device(): out_mine = lax.all_gather(out_weight, 'dp', axis=1, tiled=True)]
    all_gather x1, waiting for transfers between devices: 0.02 us -> 130 us  [per_device(): qkv_mine = lax.all_gather(qkv_weight, 'dp', axis=1, tiled=True)]
    all_to_all x0 -> x2, waiting for transfers between devices: none -> 76.4 us  [the longest x1 76.4 us: per_device(): lax.all_to_all(jnp.stack([out_weight] * lax.axis_size('dp')), 'dp', 0, 0)]
    all_gather x1, waiting for transfers between devices: 0.02 us -> 31.4 us  [per_device(): out_full = lax.all_gather(out_mine, 'fsdp', axis=0, tiled=True)]
    all_to_all x0 -> x2, starting transfers between devices: none -> 25.9 us  [the longest x1 21.8 us: per_device(): lax.all_to_all(jnp.stack([out_weight] * lax.axis_size('dp')), 'dp', 0, 0)]
    all_gather x1, waiting for transfers between devices: 210 us -> 222 us  [per_device(): part_rows = lax.all_gather(merge_weight, 'dp', axis=0, tiled=True)]
    all_to_all x1 -> x0, blocking collectives: 9.11 us -> none  [per_device(): lax.all_to_all(blocks, 'fsdp', split_axis=2, concat_axis=0, tiled=True)]
  transfers between devices with their start and end apart: 6 -> 8, of which waited for: 3 -> 7; matrix products, arithmetic and copies ran while one was open for 7% -> 8% of each run, Pallas kernels for 0% -> 0%
where the time goes in v1:
time: 659 us; the launch traced here: 658 us
  waiting for transfers between devices  491 us (75%)
  blocking collectives  63.4 us (10%)
  local copies, waits for them, and re-layouts  43.7 us (7%)
  starting transfers between devices  29.7 us (5%)
  between operations  13.5 us (2%)
  matrix products  12.3 us (2%)
    all_gather x1, waiting for transfers between devices, per_device(): part_rows = lax.all_gather(merge_weight, 'dp', axis=0, tiled=True)  222 us
    all_gather x1, waiting for transfers between devices, per_device(): qkv_mine = lax.all_gather(qkv_weight, 'dp', axis=1, tiled=True)  130 us
    all_to_all x1, waiting for transfers between devices, per_device(): lax.all_to_all(jnp.stack([out_weight] * lax.axis_size('dp')), 'dp', 0, 0)  76.4 us
    all_to_all x1, blocking collectives, per_device(): lax.all_to_all(packed, 'dp', split_axis=0, concat_axis=0, tiled=True)  58.4 us
    all_gather x1, waiting for transfers between devices, per_device(): out_full = lax.all_gather(out_mine, 'fsdp', axis=0, tiled=True)  31.4 us
    all_to_all x1, starting transfers between devices, per_device(): lax.all_to_all(jnp.stack([out_weight] * lax.axis_size('dp')), 'dp', 0, 0)  21.8 us
    reduce_scatter x1, waiting for transfers between devices, per_device(): lax.psum_scatter(jnp.dot(gathered_inputs, part_rows, preferred_element_ty...  19.2 us
    unnamed x19, local copies, waits for them, and re-layouts  18.4 us
  transfers between devices with their start and end apart: 8, of which 7 were waited for; matrix products, arithmetic and copies ran while one was open for 8% of the time, Pallas kernels for 0%

profile of v1, /device:TPU:32, one launch (start us, length us, event | category | flops | bytes accessed | tf_op | source)
XLA Modules:
  0.0 658.4 jit_solution(1961856393388038050)
XLA Ops:
  6.5 0.7 all-gather.8.cloned.1.call-update
  7.3 2.0 stack.2
  9.3 21.8 %all-to-all-start.1 = ((bf16[128,320,10]{1,2,0:T(8,128)(2,1)}), bf16[128,320,10]{1,2,0:T(8,128)(2,1)S(1)}, u32[]{:S(2)}, u32[]{:S(2)}) async-start(bf16[128,320,10]{1,2,0:T(8,128)(2,1)} %stack.2), calls=%async_computation.1 | async-start | bytes 3145728 | tf_op jit(solution)/shard_map/all_to_all | solution.py:54
  31.5 1.0 fusion.25
  32.6 76.4 %all-to-all-done.1 = bf16[128,320,10]{1,2,0:T(8,128)(2,1)S(1)} async-done(((bf16[128,320,10]{1,2,0:T(8,128)(2,1)}), bf16[128,320,10]{1,2,0:T(8,128)(2,1)S(1)}, u32[]{:S(2)}, u32[]{:S(2)}) %all-to-all-start.1) | async-done | bytes 819232 | tf_op jit(solution)/shard_map/all_to_all | solution.py:54
  108.9 0.6 reshape.109
  109.6 1.3 copy.24
  110.9 0.5 all-gather.12.cloned.1.call-update
  111.5 5.0 all_gather.15
  116.5 0.5 broadcast.115
  117.0 0.6 reduce.7
  118.0 130.0 %all-gather.8.cloned.1.call-done = bf16[3,1280,320]{2,0,1:T(4,128)(2,1)} async-done(((bf16[3,10,320]{2,0,1:T(4,128)(2,1)}), bf16[3,1280,320]{2,0,1:T(4,128)(2,1)}) %all-gather.8.cloned.1.call-update) | async-done | bytes 2457616 | tf_op jit(solution)/shard_map/all_gather | solution.py:52
  248.0 10.5 %fusion.49 = (bf16[1,1280,320]{2,0,1:T(2,128)(2,1)S(1)}, bf16[1,1280,320]{2,0,1:T(2,128)(2,1)}, bf16[1,1280,320]{2,0,1:T(2,128)(2,1)}) fusion(bf16[3,1280,320]{2,0,1:T(4,128)(2,1)} %all-gather.8.cloned.1.call-done), kind=kLoop, calls=%fused_computation.92 | loop fusion | bytes 4915200 | tf_op jit(solution)/shard_map/slice | solution.py:67
  258.5 4.9 copy.29
  263.4 4.9 copy.28
  268.3 2.8 copy.27
  271.0 4.0 all-gather.6.cloned.1.call-done
  275.0 2.3 convolution_convert_fusion.3
  277.3 0.6 convolution_convert_fusion.4
  277.9 0.4 fusion.53
  278.5 0.4 fusion.52
  279.1 0.4 fusion.51
  279.7 0.4 fusion.50
  280.2 0.6 convolution_convert_fusion.2
  280.8 0.3 fusion.9
  281.1 0.3 fusion.8
  281.5 0.3 fusion.7
  281.8 0.3 fusion.6
  282.1 0.7 pad_maximum_fusion
  282.9 3.6 all-to-all-start
  286.6 6.5 all-to-all-done
  293.1 31.4 %all-gather.10.cloned.1.call-done = bf16[1280,1280]{1,0:T(8,128)(2,1)} async-done(((bf16[320,1280]{1,0:T(8,128)(2,1)}), bf16[1280,1280]{1,0:T(8,128)(2,1)}) %all-gather.10.cloned.1.call-update) | async-done | bytes 3276816 | tf_op jit(solution)/shard_map/all_gather | solution.py:72
  324.4 2.6 fusion.54
  327.5 0.9 gather_fusion
  328.4 1.9 gather.7
  330.3 0.7 broadcast_select_fusion
  331.0 1.3 copy.25
  332.3 4.1 all-to-all-start.2
  336.5 222.1 %all-gather.12.cloned.1.call-done = bf16[128,10,1280]{2,1,0:T(8,128)(2,1)} async-done(((bf16[1,10,1280]{2,1,0:T(8,128)(2,1)}), bf16[128,10,1280]{2,1,0:T(8,128)(2,1)}) %all-gather.12.cloned.1.call-update) | async-done | bytes 3276816 | tf_op jit(solution)/shard_map/all_gather | solution.py:79
  558.6 5.3 reshape.122
  563.9 2.4 copy.26
  566.3 2.7 reshape.110
  569.1 2.3 convolution_convert_fusion.1
  571.8 19.2 %reduce-scatter.2.cloned.1.call-done = bf16[32,1280]{1,0:T(8,128)(2,1)} async-done(((bf16[128,1280]{1,0:T(8,128)(2,1)}), bf16[32,1280]{1,0:T(8,128)(2,1)}) %reduce-scatter.2.cloned.1.call-update) | async-done | bytes 81936 | tf_op jit(solution)/shard_map/reduce_scatter | solution.py:83
  591.0 1.2 convolution_convert_fusion
  592.2 0.2 reshape.111
  592.4 58.4 %all_to_all.41 = bf16[128,2,1280]{2,1,0:T(2,128)(2,1)S(1)} all-to-all(bf16[128,2,1280]{2,1,0:T(2,128)(2,1)S(1)} %reshape.111), channel_id=1, replica_groups=mesh['dp'=128,'fsdp'=4] {'dp'}, dimensions={0} | all-to-all | bytes 1310720 | tf_op jit(solution)/shard_map/all_to_all | solution.py:102
  650.8 1.1 reshape.112
  (48 shorter events, 2.5 us)
Async XLA Ops:
  6.5 241.5 %all-gather.8.cloned.1.call-start = ((), (), s32[]{:S(2)}) async-start(), calls=%async_computation.6 | async-start | bytes 3962880 | tf_op jit(solution)/shard_map/all_gather | solution.py:52
  9.3 21.8 %copy-start.2 = (f32[2,1280]{1,0:T(2,128)S(1)}, f32[2,1280]{1,0:T(2,128)}, u32[]{:S(2)}) copy-start(f32[2,1280]{1,0:T(2,128)} %param.12) | copy-start | bytes 30724
  9.3 21.9 %copy-start = (bf16[128,1280]{1,0:T(8,128)(2,1)S(1)}, bf16[128,1280]{1,0:T(8,128)(2,1)}, u32[]{:S(2)}) copy-start(bf16[128,1280]{1,0:T(8,128)(2,1)} %param.8) | copy-start | bytes 983044
  9.3 99.7 %all-to-all-start.1 = ((bf16[128,320,10]{1,2,0:T(8,128)(2,1)}), bf16[128,320,10]{1,2,0:T(8,128)(2,1)S(1)}, u32[]{:S(2)}, u32[]{:S(2)}) async-start(bf16[128,320,10]{1,2,0:T(8,128)(2,1)} %stack.2), calls=%async_computation.1 | async-start | bytes 3145728 | tf_op jit(solution)/shard_map/all_to_all | solution.py:54
  31.0 244.0 %all-gather.6.cloned.1.call-start = ((), (), s32[]{:S(2)}) async-start(), calls=%async_computation.5 | async-start | bytes 1638400 | tf_op jit(solution)/shard_map/all_gather | solution.py:58
  32.5 291.9 %all-gather.10.cloned.1.call-start = ((), (), s32[]{:S(2)}) async-start(), calls=%async_computation.7 | async-start | bytes 4096000 | tf_op jit(solution)/shard_map/all_gather | solution.py:72
  109.6 1.9 copy-start.4
  109.6 7.5 %copy-start.6 = (s32[1,128]{1,0:T(1,128)S(1)}, s32[1,128]{1,0:T(1,128)}, u32[]{:S(2)}) copy-start(s32[1,128]{1,0:T(1,128)} %param.14) | copy-start | bytes 1540
  110.9 447.7 %all-gather.12.cloned.1.call-start = ((), (), s32[]{:S(2)}) async-start(), calls=%async_computation.9 | async-start | bytes 5283840 | tf_op jit(solution)/shard_map/all_gather | solution.py:79
  271.0 6.3 copy-start.1
  275.0 2.3 copy-start.5
  282.9 10.2 %all-to-all-start = ((bf16[4,128,320]{1,2,0:T(8,128)(2,1)}), bf16[4,128,320]{1,2,0:T(8,128)(2,1)S(1)}, u32[]{:S(2)}, u32[]{:S(2)}) async-start(bf16[4,128,320]{1,2,0:T(8,128)(2,1)} %pad_maximum_fusion), calls=%async_computation | async-start | bytes 655360 | tf_op jit(solution)/shard_map/all_to_all | solution.py:71
  332.3 231.6 %all-to-all-start.2 = ((bf16[32,128,40]{1,0,2:T(8,128)(2,1)}), bf16[32,128,40]{1,0,2:T(8,128)(2,1)}, u32[]{:S(2)}, u32[]{:S(2)}) async-start(bf16[32,128,40]{1,0,2:T(8,128)(2,1)} %copy.25), calls=%async_computation.2 | async-start | bytes 655360 | tf_op jit(solution)/shard_map/all_to_all | solution.py:81
  336.4 254.5 %reduce-scatter.2.cloned.1.call-start = ((), (), s32[]{:S(2)}) async-start(), calls=%async_computation.8 | async-start | bytes 409600 | tf_op jit(solution)/shard_map/reduce_scatter | solution.py:83
  569.1 2.4 copy-start.3
Sparse Core Ops, SparseCore 0:
  11.8 236.1 all-gather.7
  250.1 24.8 all-gather.5
  277.1 47.2 all-gather.9
  328.7 229.8 all-gather.11
  571.5 19.3 reduce-scatter.1
